TPU v7x, 32 devices: a whole 2x2x4 slice. The times are simulated.
32 devices in a mesh: groups: 2 (over y), seq: 4 (over z), head: 4 (over x, core).
Axes of the slice: x: 2, y: 2, z: 4, core: 2. Of those that a mesh axis runs over, the one named last changes fastest.
Arguments:
- query: bfloat16 [8192, 1536], P(('groups', 'seq', 'head')), parts along dimension 0, may hold values from -150 to 150
- key_in: bfloat16 [8192, 1536], P(('groups', 'seq', 'head')), parts along dimension 0, may hold values from -6 to 6
- value: bfloat16 [8192, 1536], P(('groups', 'seq', 'head')), parts along dimension 0, may hold values from -6 to 6
- grad_out: bfloat16 [8192, 1536], P(('groups', 'seq', 'head')), parts along dimension 0, may hold values from -6 to 6
- pattern: int32 [16, 3], replicated, may hold values from 0 to 15, as said below
- live: int32 [16, 3], replicated, may hold values from 0 to 1, as said below
Outputs:
- attended: bfloat16 [8192, 1536], P(('groups', 'seq', 'head')), parts along dimension 0
- query_grad: bfloat16 [8192, 1536], P(('groups', 'seq', 'head')), parts along dimension 0
- key_grad: bfloat16 [8192, 1536], P(('groups', 'seq', 'head')), parts along dimension 0
- value_grad: bfloat16 [8192, 1536], P(('groups', 'seq', 'head')), parts along dimension 0
There are 2 independent parts, one for each index of `groups`. A program takes and returns all parts, laid end to end along the dimension named above; an argument that names none is the same for every part. Nothing has to cross between parts.
Inputs may be any that keep to these rules, and one draw needn't show every extreme that they name: `pattern`: each entry names a tile of the same frame-tile layer as its query tile or of the layer just before or after it; the live entries of a row are distinct; an entry that is not live names the query tile itself. Slot 0 of every row is live and names the query tile itself.
All inputs are finite; a program needn't handle non-finite values.
Results may differ from a plain program's by a relative error of at most 0.015.
Values may be sent and summed in bfloat16 or wider, within the bound.
A program may use at most 128 MiB of HBM per device.

v0:
```python
import jax
import jax.numpy as jnp
from jax import lax
from jax.sharding import PartitionSpec as P

HEADS = 12
HEAD_DIM = 128


def extended_2(cells, sides, width):
    for axis, dim in sides:
        count = lax.axis_size(axis)
        ends = count - 1
        head = lax.slice_in_dim(cells, 0, width, axis=dim)
        tail = lax.slice_in_dim(cells, cells.shape[dim] - width, cells.shape[dim], axis=dim)
        cells = jnp.concatenate(
            [
                lax.ppermute(tail, axis, [(i, (i + 1) % count) for i in range(ends)]),
                cells,
                lax.ppermute(head, axis, [((i + 1) % count, i) for i in range(ends)]),
            ],
            axis=dim,
        )
    return cells


def shifted(value, axis, steps):
    count = lax.axis_size(axis)
    initial, last = (max(0, -steps), min(count, count - steps))
    return lax.ppermute(value, axis, [(source, source + steps) for source in range(initial, last)])


def head_split(rows_flat, tiles, heads):
    width = rows_flat.shape[1]
    return rows_flat.reshape(tiles, rows_flat.shape[0] // tiles, heads, width // heads).transpose(
        2, 0, 1, 3
    )


def head_join(blocks):
    heads, tiles, tile_size, head_size = blocks.shape
    return blocks.transpose(1, 2, 0, 3).reshape(tiles * tile_size, heads * head_size)


def forward_head(q_tile, g_tile, k_all, v_all, tile_ids, alive, scale):
    k_sel = k_all[tile_ids]
    v_sel = v_all[tile_ids]
    scores = jnp.einsum("aqd,ankd->aqnk", q_tile, k_sel, preferred_element_type=jnp.float32) * scale
    scores = jnp.where(alive[:, None, :, None], scores, -jnp.inf)
    peak = jnp.max(scores, axis=(2, 3), keepdims=True)
    exponent = jnp.exp(scores - peak)
    total = jnp.sum(exponent, axis=(2, 3), keepdims=True)
    weights = exponent / total
    weights_low = weights.astype(jnp.bfloat16)
    attended = jnp.einsum(
        "aqnk,ankd->aqd", weights_low, v_sel, preferred_element_type=jnp.float32
    ).astype(jnp.bfloat16)
    weight_grad = jnp.einsum("aqd,ankd->aqnk", g_tile, v_sel, preferred_element_type=jnp.float32)
    delta = jnp.sum(weights * weight_grad, axis=(2, 3), keepdims=True)
    score_grad = (weights * (weight_grad - delta) * scale).astype(jnp.bfloat16)
    query_grad = jnp.einsum(
        "aqnk,ankd->aqd", score_grad, k_sel, preferred_element_type=jnp.float32
    ).astype(jnp.bfloat16)
    onehot = (
        tile_ids[:, :, None] == jnp.arange(k_all.shape[0], dtype=jnp.int32)[None, None, :]
    ).astype(jnp.float32)
    key_slots = jnp.einsum("aqnk,aqd->ankd", score_grad, q_tile, preferred_element_type=jnp.float32)
    value_slots = jnp.einsum(
        "aqnk,aqd->ankd", weights_low, g_tile, preferred_element_type=jnp.float32
    )
    key_sums = jnp.einsum("anj,ankd->jkd", onehot, key_slots, precision=lax.Precision.HIGHEST)
    value_sums = jnp.einsum("anj,ankd->jkd", onehot, value_slots, precision=lax.Precision.HIGHEST)
    return (attended, query_grad, key_sums, value_sums)


def body(query, key_in, value, grad_out, pattern, live):
    members = lax.axis_size("head")
    heads = HEADS // members
    scale = HEAD_DIM ** (-0.5)
    queries, keys, values, out_grads = (
        lax.all_to_all(query, "head", split_axis=1, concat_axis=0, tiled=True),
        lax.all_to_all(key_in, "head", split_axis=1, concat_axis=0, tiled=True),
        lax.all_to_all(value, "head", split_axis=1, concat_axis=0, tiled=True),
        lax.all_to_all(grad_out, "head", split_axis=1, concat_axis=0, tiled=True),
    )
    tile_size = queries.shape[0] // members
    margin = members * tile_size
    seq_index = lax.axis_index("seq")
    first = seq_index * members
    extended = extended_2(jnp.stack([keys, values]), (("seq", 1),), margin)
    rows = lax.dynamic_slice_in_dim(pattern, first, members, 0)
    alive_rows = lax.dynamic_slice_in_dim(live, first, members, 0)
    tile_ids = rows - first + members
    alive = alive_rows > 0
    q_heads = head_split(queries, members, heads)
    g_heads = head_split(out_grads, members, heads)
    k_heads = head_split(extended[0], 3 * members, heads)
    v_heads = head_split(extended[1], 3 * members, heads)

    def with_partials(operands):
        return forward_head(
            operands[0], operands[1], operands[2], operands[3], tile_ids, alive, scale
        )

    attended, query_grad, key_sums, value_sums = lax.map(
        with_partials, (q_heads, g_heads, k_heads, v_heads)
    )
    grads = jnp.stack([head_join(key_sums), head_join(value_sums)])
    from_above = shifted(grads[:, :margin].astype(jnp.bfloat16), "seq", -1).astype(jnp.float32)
    from_below = shifted(grads[:, 2 * margin :].astype(jnp.bfloat16), "seq", 1).astype(jnp.float32)
    owned = grads[:, margin : 2 * margin] + from_above + from_below
    key_own = owned[0]
    value_own = owned[1]
    result = (
        lax.all_to_all(head_join(attended), "head", split_axis=0, concat_axis=1, tiled=True),
        lax.all_to_all(head_join(query_grad), "head", split_axis=0, concat_axis=1, tiled=True),
        lax.all_to_all(
            key_own.astype(jnp.bfloat16), "head", split_axis=0, concat_axis=1, tiled=True
        ),
        lax.all_to_all(
            value_own.astype(jnp.bfloat16), "head", split_axis=0, concat_axis=1, tiled=True
        ),
    )
    return (result[0], result[1], result[2], result[3])


def solution(mesh):
    placed = (
        P(("groups", "seq", "head"), None),
        P(("groups", "seq", "head"), None),
        P(("groups", "seq", "head"), None),
        P(("groups", "seq", "head"), None),
        P(),
        P(),
    )
    return jax.shard_map(
        body,
        mesh=mesh,
        in_specs=placed,
        out_specs=(
            P(("groups", "seq", "head"), None),
            P(("groups", "seq", "head"), None),
            P(("groups", "seq", "head"), None),
            P(("groups", "seq", "head"), None),
        ),
        check_vma=False,
    )
```

profile of v0, /device:TPU:24, one launch (start us, length us, event | category | flops | bytes accessed | tf_op | source)
XLA Modules:
  0.0 323.6 jit_solution(741371311791878829)
XLA Ops:
  7.7 10.5 %all-to-all-done.1 = bf16[256,4,384]{0,2,1:T(8,128)(2,1)S(1)} async-done(((bf16[256,4,384]{0,2,1:T(8,128)(2,1)}), bf16[256,4,384]{0,2,1:T(8,128)(2,1)S(1)}, u32[]{:S(2)}, u32[]{:S(2)}) %all-to-all-start.1) | async-done | bytes 786464 | tf_op jit(solution)/shard_map/all_to_all | solution.py:82
  22.0 11.2 %all-to-all-done.2 = bf16[256,4,384]{0,2,1:T(8,128)(2,1)S(1)} async-done(((bf16[256,4,384]{0,2,1:T(8,128)(2,1)}), bf16[256,4,384]{0,2,1:T(8,128)(2,1)S(1)}, u32[]{:S(2)}, u32[]{:S(2)}) %all-to-all-start.2) | async-done | bytes 786464 | tf_op jit(solution)/shard_map/all_to_all | solution.py:83
  45.9 25.2 %collective-permute-done.1 = bf16[2,1024,384]{2,1,0:T(8,128)(2,1)} collective-permute-done((bf16[2,1024,384]{2,1,0:T(8,128)(2,1)}, bf16[2,1024,384]{2,1,0:T(8,128)(2,1)}, u32[]{:S(2)}, u32[]{:S(2)}) %collective-permute-start.1) | collective-permute-done | bytes 1572896 | tf_op jit(solution)/shard_map/ppermute | solution.py:20
  71.1 5.2 %collective-permute-done = bf16[2,1024,384]{2,1,0:T(8,128)(2,1)} collective-permute-done((bf16[2,1024,384]{2,1,0:T(8,128)(2,1)}, bf16[2,1024,384]{2,1,0:T(8,128)(2,1)}, u32[]{:S(2)}, u32[]{:S(2)}) %collective-permute-start) | collective-permute-done | bytes 1572896 | tf_op jit(solution)/shard_map/ppermute | solution.py:18
  76.3 4.6 %pad_maximum_fusion = bf16[2,3072,384]{2,1,0:T(8,128)(2,1)} fusion(bf16[2,1024,384]{2,1,0:T(8,128)(2,1)} %collective-permute-done.1, bf16[1,1024,384]{2,1,0:T(8,128)(2,1)S(1)} %bitcast.172, bf16[1,1024,384]{2,1,0:T(8,128)(2,1)S(1)} %bitcast.170, bf16[2,1024,384]{2,1,0:T(8,128)(2,1)} %collective-permute-done), kind=kLoop, calls=%fused_computation.47 | loop fusion | flops 18874368 | bytes 9437184 | tf_op jit(solution)/shard_map/concatenate | solution.py:16
  81.0 4.2 %all-to-all-start.3 = ((bf16[256,4,384]{0,2,1:T(8,128)(2,1)}), bf16[256,4,384]{0,2,1:T(8,128)(2,1)}, u32[]{:S(2)}, u32[]{:S(2)}) async-start(bf16[256,4,384]{0,2,1:T(8,128)(2,1)} %bitcast.38), calls=%async_computation.3 | async-start | bytes 1572864 | tf_op jit(solution)/shard_map/all_to_all | solution.py:84
  85.2 4.3 %fusion.37 = (bf16[1,3072,384]{2,1,0:T(8,128)(2,1)}, bf16[1,3072,384]{2,1,0:T(8,128)(2,1)S(1)}) fusion(bf16[2,3072,384]{2,1,0:T(8,128)(2,1)} %pad_maximum_fusion), kind=kLoop, calls=%fused_computation.59 | loop fusion | bytes 9437184 | tf_op jit(solution)/shard_map/slice | solution.py:98
  89.4 4.3 %copy.49 = bf16[1,3072,384]{1,2,0:T(8,128)(2,1)} copy(bf16[1,3072,384]{2,1,0:T(8,128)(2,1)} %get-tuple-element.128) | data formatting | bytes 4718592 | tf_op jit(solution)/shard_map/slice | solution.py:98
  93.7 5.4 %reshape_squeeze.7 = bf16[12,256,3,128]{1,0,3,2:T(8,128)(2,1)} reshape(bf16[1,3072,384]{1,2,0:T(8,128)(2,1)} %copy.49) | data formatting | bytes 4718592 | tf_op jit(solution)/shard_map/reshape;squeeze | solution.py:35
  99.1 4.8 %copy.53 = bf16[3,12,256,128]{3,2,1,0:T(8,128)(2,1)} copy(bf16[3,12,256,128]{2,1,3,0:T(8,128)(2,1)} %bitcast.167) | data formatting | bytes 4718592 | tf_op jit(solution)/shard_map/while | solution.py:105
  106.6 5.4 %reshape_squeeze.6 = bf16[12,256,3,128]{1,0,3,2:T(8,128)(2,1)} reshape(bf16[1,3072,384]{1,2,0:T(8,128)(2,1)} %copy.47) | data formatting | bytes 4718592 | tf_op jit(solution)/shard_map/reshape;squeeze | solution.py:35
  112.0 4.8 %copy.52 = bf16[3,12,256,128]{3,2,1,0:T(8,128)(2,1)} copy(bf16[3,12,256,128]{2,1,3,0:T(8,128)(2,1)} %bitcast.168) | data formatting | bytes 4718592 | tf_op jit(solution)/shard_map/while | solution.py:105
  116.8 92.5 %while.16 = (s32[]{:T(128)}, bf16[3,4,256,128]{2,3,0,1:T(8,128)(2,1)}, bf16[3,4,256,128]{2,3,0,1:T(8,128)(2,1)}, f32[3,12,256,128]{3,1,2,0:T(8,128)}, f32[3,12,2...) while((s32[]{:T(128)}, ...), condition=%wide.region_4.5_spmd, body=%wide.region_0.4_spmd.sunk | while | flops 1345845504 | bytes 75555744 | solution.py:105
  143.7 4.0 %bitcast_dynamic-update-slice_fusion.5 = f32[3,12,256,128]{3,1,2,0:T(8,128)} fusion(f32[3,12,256,128]{3,1,2,0:T(8,128)} %get-tuple-element.229, s32[]{:T(128)S(6)} %copy.106, f32[4,3,256,128]{3,2,1,0:T(8,128)S(1)} %copy-done.1, s32[4,3]{0,1:T(4,128)S(1)} %copy.96), kind=kOutput, calls=%fused_computation.9.clone.1 | convolution fusion | flops 56623248 | bytes 3670068 | tf_op jit(solution)/shard_map/while/body/eval_jaxpr/anj,ankd->jkd/dot_general | solution.py:72
  174.5 4.0 %bitcast_dynamic-update-slice_fusion.5 = f32[3,12,256,128]{3,1,2,0:T(8,128)} fusion(f32[3,12,256,128]{3,1,2,0:T(8,128)} %get-tuple-element.229, s32[]{:T(128)S(6)} %copy.106, f32[4,3,256,128]{3,2,1,0:T(8,128)S(1)} %copy-done.1, s32[4,3]{0,1:T(4,128)S(1)} %copy.96), kind=kOutput, calls=%fused_computation.9.clone.1 | convolution fusion | flops 56623248 | bytes 3670068 | tf_op jit(solution)/shard_map/while/body/eval_jaxpr/anj,ankd->jkd/dot_general | solution.py:72
  209.4 6.8 %copy.58 = f32[12,256,3,128]{1,0,3,2:T(8,128)} copy(f32[12,256,3,128]{3,0,1,2:T(8,128)} %bitcast.173) | data formatting | bytes 9437184 | tf_op jit(solution)/shard_map/transpose | solution.py:42
  216.2 6.9 %stack_reshape.7 = f32[1,3072,384]{1,2,0:T(8,128)} reshape(f32[12,256,3,128]{1,0,3,2:T(8,128)} %copy.58) | data formatting | bytes 9437184 | tf_op jit(solution)/shard_map/stack;reshape | solution.py:108
  223.0 6.7 %copy.57 = f32[12,256,3,128]{1,0,3,2:T(8,128)} copy(f32[12,256,3,128]{3,0,1,2:T(8,128)} %bitcast.174) | data formatting | bytes 9437184 | tf_op jit(solution)/shard_map/transpose | solution.py:42
  229.7 6.9 %stack_reshape.6 = f32[1,3072,384]{1,2,0:T(8,128)} reshape(f32[12,256,3,128]{1,0,3,2:T(8,128)} %copy.57) | data formatting | bytes 9437184 | tf_op jit(solution)/shard_map/stack;reshape | solution.py:108
  249.7 14.7 %all_to_all.134 = bf16[4,256,384]{1,2,0:T(8,128)(2,1)S(1)} all-to-all(bf16[4,256,384]{1,2,0:T(8,128)(2,1)S(1)} %bitcast.184), channel_id=1, replica_groups=mesh['groups'=2,'seq'=4,'head'=4] {'head'}, dimensions={0} | all-to-all | bytes 1572864 | tf_op jit(solution)/shard_map/all_to_all | solution.py:115
  267.9 14.0 %collective-permute-done.2 = bf16[2,1024,384]{1,2,0:T(8,128)(2,1)} collective-permute-done((bf16[2,1024,384]{1,2,0:T(8,128)(2,1)}, bf16[2,1024,384]{1,2,0:T(8,128)(2,1)}, u32[]{:S(2)}, u32[]{:S(2)}) %collective-permute-start.2) | collective-permute-done | bytes 1572896 | tf_op jit(solution)/shard_map/ppermute | solution.py:30
  281.9 5.1 %collective-permute-done.3 = bf16[2,1024,384]{1,2,0:T(8,128)(2,1)} collective-permute-done((bf16[2,1024,384]{1,2,0:T(8,128)(2,1)S(1)}, bf16[2,1024,384]{1,2,0:T(8,128)(2,1)}, u32[]{:S(2)}, u32[]{:S(2)}) %collective-permute-start.3) | collective-permute-done | bytes 1572896 | tf_op jit(solution)/shard_map/ppermute | solution.py:30
  296.6 10.5 %all-to-all-done.7 = bf16[4,256,384]{2,1,0:T(8,128)(2,1)S(1)} async-done(((bf16[4,256,384]{2,1,0:T(8,128)(2,1)}), bf16[4,256,384]{2,1,0:T(8,128)(2,1)S(1)}, u32[]{:S(2)}, u32[]{:S(2)}) %all-to-all-start.7) | async-done | bytes 786464 | tf_op jit(solution)/shard_map/all_to_all | solution.py:120
  314.3 7.9 %all-to-all-done.6 = bf16[4,256,384]{2,1,0:T(8,128)(2,1)S(1)} async-done(((bf16[4,256,384]{2,1,0:T(8,128)(2,1)}), bf16[4,256,384]{2,1,0:T(8,128)(2,1)S(1)}, u32[]{:S(2)}, u32[]{:S(2)}) %all-to-all-start.6) | async-done | bytes 786464 | tf_op jit(solution)/shard_map/all_to_all | solution.py:117
  (157 shorter events, 145.2 us)
Async XLA Ops:
  0.6 5.9 %copy-start.8 = (bf16[256,1536]{1,0:T(8,128)(2,1)S(1)}, bf16[256,1536]{1,0:T(8,128)(2,1)}, u32[]{:S(2)}) copy-start(bf16[256,1536]{1,0:T(8,128)(2,1)} %param.10) | copy-start | bytes 2359300
  3.0 15.1 %all-to-all-start.1 = ((bf16[256,4,384]{0,2,1:T(8,128)(2,1)}), bf16[256,4,384]{0,2,1:T(8,128)(2,1)S(1)}, u32[]{:S(2)}, u32[]{:S(2)}) async-start(bf16[256,4,384]{0,2,1:T(8,128)(2,1)} %bitcast.30), calls=%async_computation.1 | async-start | bytes 1572864 | tf_op jit(solution)/shard_map/all_to_all | solution.py:82
  18.1 15.1 %all-to-all-start.2 = ((bf16[256,4,384]{0,2,1:T(8,128)(2,1)}), bf16[256,4,384]{0,2,1:T(8,128)(2,1)S(1)}, u32[]{:S(2)}, u32[]{:S(2)}) async-start(bf16[256,4,384]{0,2,1:T(8,128)(2,1)} %bitcast.33), calls=%async_computation.2 | async-start | bytes 1572864 | tf_op jit(solution)/shard_map/all_to_all | solution.py:83
  22.0 17.8 %copy-start.9 = (bf16[256,1536]{1,0:T(8,128)(2,1)S(1)}, bf16[256,1536]{1,0:T(8,128)(2,1)}, u32[]{:S(2)}) copy-start(bf16[256,1536]{1,0:T(8,128)(2,1)} %param.8) | copy-start | bytes 2359300
  33.6 10.9 %copy-start.12 = (s32[16,3]{0,1:T(4,128)S(1)}, s32[16,3]{0,1:T(4,128)}, u32[]{:S(2)}) copy-start(s32[16,3]{0,1:T(4,128)} %param.12) | copy-start | bytes 580
  33.6 10.9 %copy-start.13 = (s32[16,3]{0,1:T(4,128)S(1)}, s32[16,3]{0,1:T(4,128)}, u32[]{:S(2)}) copy-start(s32[16,3]{0,1:T(4,128)} %param.13) | copy-start | bytes 580
  33.6 11.1 %copy-start.10 = (bf16[256,1536]{1,0:T(8,128)(2,1)S(1)}, bf16[256,1536]{1,0:T(8,128)(2,1)}, u32[]{:S(2)}) copy-start(bf16[256,1536]{1,0:T(8,128)(2,1)} %param.11) | copy-start | bytes 2359300
  35.0 36.1 %collective-permute-start.1 = (bf16[2,1024,384]{2,1,0:T(8,128)(2,1)}, bf16[2,1024,384]{2,1,0:T(8,128)(2,1)}, u32[]{:S(2)}, u32[]{:S(2)}) collective-permute-start(bf16[2,1024,384]{2,1,0:T(8,128)(2,1)} %pad_maximum_fusion.1), channel_id=1, source_target_pairs={{4,0},{8,4},{12,8},{5,1},{9,5},{13,9},{6,2},{10,6},{14,10},{7,3},{... | collective-permute-start | bytes 4718600 | tf_op jit(solution)/shard_map/ppermute | solution.py:20
  38.5 37.9 %collective-permute-start = (bf16[2,1024,384]{2,1,0:T(8,128)(2,1)}, bf16[2,1024,384]{2,1,0:T(8,128)(2,1)}, u32[]{:S(2)}, u32[]{:S(2)}) collective-permute-start(bf16[2,1024,384]{2,1,0:T(8,128)(2,1)} %pad_maximum_fusion.1), channel_id=1, source_target_pairs={{0,4},{4,8},{8,12},{1,5},{5,9},{9,13},{2,6},{6,10},{10,14},{3,7},{... | collective-permute-start | bytes 4718600 | tf_op jit(solution)/shard_map/ppermute | solution.py:18
  40.9 40.1 %all-to-all-start = ((bf16[256,4,384]{0,2,1:T(8,128)(2,1)}), bf16[256,4,384]{0,2,1:T(8,128)(2,1)S(1)}, u32[]{:S(2)}, u32[]{:S(2)}) async-start(bf16[256,4,384]{0,2,1:T(8,128)(2,1)} %bitcast.26), calls=%async_computation | async-start | bytes 1572864 | tf_op jit(solution)/shard_map/all_to_all | solution.py:81
  81.0 35.9 %all-to-all-start.3 = ((bf16[256,4,384]{0,2,1:T(8,128)(2,1)}), bf16[256,4,384]{0,2,1:T(8,128)(2,1)}, u32[]{:S(2)}, u32[]{:S(2)}) async-start(bf16[256,4,384]{0,2,1:T(8,128)(2,1)} %bitcast.38), calls=%async_computation.3 | async-start | bytes 1572864 | tf_op jit(solution)/shard_map/all_to_all | solution.py:84
  137.1 6.5 %copy-start.1 = (f32[4,3,256,128]{3,2,1,0:T(8,128)S(1)}, f32[4,3,256,128]{3,2,1,0:T(8,128)}, u32[]{:S(2)}) copy-start(f32[4,3,256,128]{3,2,1,0:T(8,128)} %fusion.84) | copy-start | bytes 4718596 | tf_op jit(solution)/shard_map/while
  143.7 4.0 %copy-start.7 = (bf16[3,4,256,128]{2,3,0,1:T(8,128)(2,1)S(1)}, bf16[3,4,256,128]{2,3,0,1:T(8,128)(2,1)}, u32[]{:S(2)}) copy-start(bf16[3,4,256,128]{2,3,0,1:T(8,128)(2,1)} %copy-done.6) | copy-start | bytes 2359300 | tf_op jit(solution)/shard_map/while
  168.0 6.5 %copy-start.1 = (f32[4,3,256,128]{3,2,1,0:T(8,128)S(1)}, f32[4,3,256,128]{3,2,1,0:T(8,128)}, u32[]{:S(2)}) copy-start(f32[4,3,256,128]{3,2,1,0:T(8,128)} %fusion.84) | copy-start | bytes 4718596 | tf_op jit(solution)/shard_map/while
  174.5 4.0 %copy-start.7 = (bf16[3,4,256,128]{2,3,0,1:T(8,128)(2,1)S(1)}, bf16[3,4,256,128]{2,3,0,1:T(8,128)(2,1)}, u32[]{:S(2)}) copy-start(bf16[3,4,256,128]{2,3,0,1:T(8,128)(2,1)} %copy-done.6) | copy-start | bytes 2359300 | tf_op jit(solution)/shard_map/while
  198.8 6.6 %copy-start.1 = (f32[4,3,256,128]{3,2,1,0:T(8,128)S(1)}, f32[4,3,256,128]{3,2,1,0:T(8,128)}, u32[]{:S(2)}) copy-start(f32[4,3,256,128]{3,2,1,0:T(8,128)} %fusion.84) | copy-start | bytes 4718596 | tf_op jit(solution)/shard_map/while
  205.4 4.0 %copy-start.7 = (bf16[3,4,256,128]{2,3,0,1:T(8,128)(2,1)S(1)}, bf16[3,4,256,128]{2,3,0,1:T(8,128)(2,1)}, u32[]{:S(2)}) copy-start(bf16[3,4,256,128]{2,3,0,1:T(8,128)(2,1)} %copy-done.6) | copy-start | bytes 2359300 | tf_op jit(solution)/shard_map/while
  236.5 3.8 %copy-start.5 = (f32[1,3072,384]{1,2,0:T(8,128)S(1)}, f32[1,3072,384]{1,2,0:T(8,128)}, u32[]{:S(2)}) copy-start(f32[1,3072,384]{1,2,0:T(8,128)} %stack_reshape.7) | copy-start | bytes 14155780
  244.3 5.4 %copy-start.11 = (bf16[3,4,256,128]{2,3,0,1:T(8,128)(2,1)S(1)}, bf16[3,4,256,128]{2,3,0,1:T(8,128)(2,1)}, u32[]{:S(2)}) copy-start(bf16[3,4,256,128]{2,3,0,1:T(8,128)(2,1)} %get-tuple-element.64) | copy-start | bytes 2359300
  245.8 36.1 %collective-permute-start.2 = (bf16[2,1024,384]{1,2,0:T(8,128)(2,1)}, bf16[2,1024,384]{1,2,0:T(8,128)(2,1)}, u32[]{:S(2)}, u32[]{:S(2)}) collective-permute-start(bf16[2,1024,384]{1,2,0:T(8,128)(2,1)} %get-tuple-element.126), channel_id=1, source_target_pairs={{4,0},{8,4},{12,8},{5,1},{9,5},{13,9},{6,2},{10,6},{14,10},{7,3},{... | collective-permute-start | bytes 4718600 | tf_op jit(solution)/shard_map/ppermute | solution.py:30
  248.4 38.6 %collective-permute-start.3 = (bf16[2,1024,384]{1,2,0:T(8,128)(2,1)S(1)}, bf16[2,1024,384]{1,2,0:T(8,128)(2,1)}, u32[]{:S(2)}, u32[]{:S(2)}) collective-permute-start(bf16[2,1024,384]{1,2,0:T(8,128)(2,1)S(1)} %get-tuple-element.127), channel_id=1, source_target_pairs={{0,4},{4,8},{8,12},{1,5},{5,9},{9,13},{2,6},{6,10},{10,14},{3,7},{... | collective-permute-start | bytes 4718600 | tf_op jit(solution)/shard_map/ppermute | solution.py:30
  264.4 27.6 %all-to-all-start.5 = ((bf16[4,256,384]{1,2,0:T(8,128)(2,1)}), bf16[4,256,384]{1,2,0:T(8,128)(2,1)S(1)}, u32[]{:S(2)}, u32[]{:S(2)}) async-start(bf16[4,256,384]{1,2,0:T(8,128)(2,1)} %bitcast.183), calls=%async_computation.5 | async-start | bytes 1572864 | tf_op jit(solution)/shard_map/all_to_all | solution.py:116
  292.0 15.1 %all-to-all-start.7 = ((bf16[4,256,384]{2,1,0:T(8,128)(2,1)}), bf16[4,256,384]{2,1,0:T(8,128)(2,1)S(1)}, u32[]{:S(2)}, u32[]{:S(2)}) async-start(bf16[4,256,384]{2,1,0:T(8,128)(2,1)} %bitcast.55), calls=%async_computation.7 | async-start | bytes 1572864 | tf_op jit(solution)/shard_map/all_to_all | solution.py:120
  307.1 15.1 %all-to-all-start.6 = ((bf16[4,256,384]{2,1,0:T(8,128)(2,1)}), bf16[4,256,384]{2,1,0:T(8,128)(2,1)S(1)}, u32[]{:S(2)}, u32[]{:S(2)}) async-start(bf16[4,256,384]{2,1,0:T(8,128)(2,1)} %bitcast.52), calls=%async_computation.6 | async-start | bytes 1572864 | tf_op jit(solution)/shard_map/all_to_all | solution.py:117
  (13 other events, 26.6 us)
where the time goes:
time: 326 us; the launch traced here: 324 us
  local copies, waits for them, and re-layouts  111 us (34%)
  waiting for transfers between devices  89.5 us (27%)
  matrix products  57.4 us (18%)
  starting transfers between devices  33.8 us (10%)
  other arithmetic  15.9 us (5%)
  blocking collectives  14.7 us (5%)
    ppermute x1, waiting for transfers between devices, extended_2(): lax.ppermute(head, axis, [((i + 1) % count, i) for i in range(ends)])  25.2 us
    ppermute x2, waiting for transfers between devices, shifted(): lax.ppermute(value, axis, [(source, source + steps) for source in range(i...  19.1 us
    unnamed x27, local copies, waits for them, and re-layouts  17.3 us
    all_to_all x1, blocking collectives, body(): lax.all_to_all(head_join(attended), 'head', split_axis=0, concat_axis=1,...  14.7 us
    another operation x3, local copies, waits for them, and re-layouts, body(): grads = jnp.stack([head_join(key_sums), head_join(value_sums)])  14 us
    transpose x2, local copies, waits for them, and re-layouts, head_join(): blocks.transpose(1, 2, 0, 3).reshape(tiles * tile_size, heads * head_size)  13.5 us
    dynamic_update_slice x12, local copies, waits for them, and re-layouts, body(): lax.map(with_partials, (q_heads, g_heads, k_heads, v_heads))  13 us
    dot_general x3, matrix products, forward_head(): jnp.einsum('anj,ankd->jkd', onehot, value_slots, precision=lax.Precision....  12.1 us
  transfers between devices with their start and end apart: 11, of which 8 were waited for; matrix products, arithmetic and copies ran while one was open for 16% of the time, Pallas kernels for 0%

commit v1 on v0

--- a/solution.py
+++ b/solution.py
@@ -5,6 +5,29 @@
 
 HEADS = 12
 HEAD_DIM = 128
+
+
+def in_blocks(x, dim, devices):
+    before, after = (x.shape[:dim], x.shape[dim + 1 :])
+    return jnp.moveaxis(x.reshape(*before, devices, -1, *after), dim, 0)
+
+
+def laid_out(parts, dim):
+    lengths = list(parts.shape[1:])
+    lengths[dim] *= parts.shape[0]
+    return jnp.moveaxis(parts, 0, dim).reshape(lengths)
+
+
+def rotated_exchange(value, axis, split_dim, concat_dim):
+    size, index = (lax.axis_size(axis), lax.axis_index(axis))
+    pieces = in_blocks(value, split_dim, size)
+    out = pieces
+    for hop in range(1, size):
+        target, source = ((index + hop) % size, (index - hop) % size)
+        sent = lax.dynamic_index_in_dim(pieces, target, 0)
+        other = lax.ppermute(sent, axis, [(i, (i + hop) % size) for i in range(size)])
+        out = lax.dynamic_update_slice_in_dim(out, other, source, axis=0)
+    return laid_out(out, concat_dim)
 
 
 def extended_2(cells, sides, width):
@@ -112,7 +135,7 @@
     key_own = owned[0]
     value_own = owned[1]
     result = (
-        lax.all_to_all(head_join(attended), "head", split_axis=0, concat_axis=1, tiled=True),
+        rotated_exchange(head_join(attended), "head", 0, 1),
         lax.all_to_all(head_join(query_grad), "head", split_axis=0, concat_axis=1, tiled=True),
         lax.all_to_all(
             key_own.astype(jnp.bfloat16), "head", split_axis=0, concat_axis=1, tiled=True

time: 326 us -> 355 us (1.089); the launches traced: 324 us -> 349 us
  waiting for transfers between devices: 89.5 us -> 105 us
  blocking collectives: 14.7 us -> 0 us
  local copies, waits for them, and re-layouts: 111 us -> 120 us
  matrix products: 57.4 us -> 63.6 us
  starting transfers between devices: 33.8 us -> 39.3 us
  other arithmetic: 15.9 us -> 19.6 us
    all_to_all x1 -> x0, blocking collectives: 14.7 us -> none  [body(): lax.all_to_all(head_join(attended), 'head', split_axis=0, concat_axis=1,...]
    ppermute x0 -> x3, waiting for transfers between devices: none -> 13.2 us  [rotated_exchange(): lax.ppermute(sent, axis, [(i, (i + hop) % size) for i in range(size)])]
    all_to_all x1, waiting for transfers between devices: 10.5 us -> 0.01 us  [body(): lax.all_to_all(value_own.astype(jnp.bfloat16), 'head', split_axis=0, conc...]
    ppermute x2, waiting for transfers between devices: 19.1 us -> 29.3 us  [shifted(): lax.ppermute(value, axis, [(source, source + steps) for source in range(i...]
    dot_general x3, matrix products: 4.59 us -> 9.4 us  [forward_head(): jnp.einsum('aqnk,aqd->ankd', score_grad, q_tile, preferred_element_type=j...]
    another operation x3, local copies, waits for them, and re-layouts: 14 us -> 18.8 us  [body(): grads = jnp.stack([head_join(key_sums), head_join(value_sums)])]
    dot_general x3, matrix products: 12 us -> 16.2 us  [forward_head(): jnp.einsum('anj,ankd->jkd', onehot, key_slots, precision=lax.Precision.HI...]
    while x36 -> x30, local copies, waits for them, and re-layouts: 2.2 us -> 6.24 us
  transfers between devices with their start and end apart: 11 -> 14, of which waited for: 8 -> 8; matrix products, arithmetic and copies ran while one was open for 16% -> 15% of each run, Pallas kernels for 0% -> 0%
where the time goes in v1:
time: 355 us; the launch traced here: 349 us
  local copies, waits for them, and re-layouts  120 us (34%)
  waiting for transfers between devices  105 us (30%)
  matrix products  63.6 us (18%)
  starting transfers between devices  39.3 us (11%)
  other arithmetic  19.6 us (6%)
    ppermute x2, waiting for transfers between devices, shifted(): lax.ppermute(value, axis, [(source, source + steps) for source in range(i...  29.3 us
    ppermute x1, waiting for transfers between devices, extended_2(): lax.ppermute(head, axis, [((i + 1) % count, i) for i in range(ends)])  25.2 us
    another operation x3, local copies, waits for them, and re-layouts, body(): grads = jnp.stack([head_join(key_sums), head_join(value_sums)])  18.8 us
    dot_general x3, matrix products, forward_head(): jnp.einsum('anj,ankd->jkd', onehot, key_slots, precision=lax.Precision.HI...  16.2 us
    unnamed x23, local copies, waits for them, and re-layouts  15.8 us
    transpose x2, local copies, waits for them, and re-layouts, head_join(): blocks.transpose(1, 2, 0, 3).reshape(tiles * tile_size, heads * head_size)  13.5 us
    ppermute x3, waiting for transfers between devices, rotated_exchange(): lax.ppermute(sent, axis, [(i, (i + hop) % size) for i in range(size)])  13.2 us
    dynamic_update_slice x12, local copies, waits for them, and re-layouts, body(): lax.map(with_partials, (q_heads, g_heads, k_heads, v_heads))  13 us
  transfers between devices with their start and end apart: 14, of which 8 were waited for; matrix products, arithmetic and copies ran while one was open for 15% of the time, Pallas kernels for 0%

profile of v1, /device:TPU:24, one launch (start us, length us, event | category | flops | bytes accessed | tf_op | source)
XLA Modules:
  0.0 348.8 jit_solution(17161123764638569950)
XLA Ops:
  7.7 10.5 %all-to-all-done.2 = bf16[256,4,384]{0,2,1:T(8,128)(2,1)S(1)} async-done(((bf16[256,4,384]{0,2,1:T(8,128)(2,1)}), bf16[256,4,384]{0,2,1:T(8,128)(2,1)S(1)}, u32[]{:S(2)}, u32[]{:S(2)}) %all-to-all-start.2) | async-done | bytes 786464 | tf_op jit(solution)/shard_map/all_to_all | solution.py:106
  22.0 11.2 %all-to-all-done.1 = bf16[256,4,384]{0,2,1:T(8,128)(2,1)S(1)} async-done(((bf16[256,4,384]{0,2,1:T(8,128)(2,1)}), bf16[256,4,384]{0,2,1:T(8,128)(2,1)S(1)}, u32[]{:S(2)}, u32[]{:S(2)}) %all-to-all-start.1) | async-done | bytes 786464 | tf_op jit(solution)/shard_map/all_to_all | solution.py:105
  45.9 25.2 %collective-permute-done.1 = bf16[2,1024,384]{2,1,0:T(8,128)(2,1)} collective-permute-done((bf16[2,1024,384]{2,1,0:T(8,128)(2,1)}, bf16[2,1024,384]{2,1,0:T(8,128)(2,1)}, u32[]{:S(2)}, u32[]{:S(2)}) %collective-permute-start.1) | collective-permute-done | bytes 1572896 | tf_op jit(solution)/shard_map/ppermute | solution.py:43
  71.1 5.2 %collective-permute-done = bf16[2,1024,384]{2,1,0:T(8,128)(2,1)} collective-permute-done((bf16[2,1024,384]{2,1,0:T(8,128)(2,1)}, bf16[2,1024,384]{2,1,0:T(8,128)(2,1)}, u32[]{:S(2)}, u32[]{:S(2)}) %collective-permute-start) | collective-permute-done | bytes 1572896 | tf_op jit(solution)/shard_map/ppermute | solution.py:41
  76.3 4.7 %pad_maximum_fusion = bf16[2,3072,384]{2,1,0:T(8,128)(2,1)} fusion(bf16[2,1024,384]{2,1,0:T(8,128)(2,1)} %collective-permute-done.1, bf16[1,1024,384]{2,1,0:T(8,128)(2,1)S(1)} %bitcast.170, bf16[1,1024,384]{2,1,0:T(8,128)(2,1)S(1)} %bitcast.172, bf16[2,1024,384]{2,1,0:T(8,128)(2,1)} %collective-permute-done), kind=kLoop, calls=%fused_computation.47 | loop fusion | flops 18874368 | bytes 9437184 | tf_op jit(solution)/shard_map/concatenate | solution.py:39
  93.7 5.4 %reshape_squeeze.6 = bf16[12,256,3,128]{1,0,3,2:T(8,128)(2,1)} reshape(bf16[1,3072,384]{1,2,0:T(8,128)(2,1)} %copy.47) | data formatting | bytes 4718592 | tf_op jit(solution)/shard_map/reshape;squeeze | solution.py:58
  99.1 4.8 %copy.52 = bf16[3,12,256,128]{3,2,1,0:T(8,128)(2,1)} copy(bf16[3,12,256,128]{2,1,3,0:T(8,128)(2,1)} %bitcast.167) | data formatting | bytes 4718592 | tf_op jit(solution)/shard_map/while | solution.py:128
  106.6 5.4 %reshape_squeeze.7 = bf16[12,256,3,128]{1,0,3,2:T(8,128)(2,1)} reshape(bf16[1,3072,384]{1,2,0:T(8,128)(2,1)} %copy.49) | data formatting | bytes 4718592 | tf_op jit(solution)/shard_map/reshape;squeeze | solution.py:58
  112.0 4.8 %copy.53 = bf16[3,12,256,128]{3,2,1,0:T(8,128)(2,1)} copy(bf16[3,12,256,128]{2,1,3,0:T(8,128)(2,1)} %bitcast.168) | data formatting | bytes 4718592 | tf_op jit(solution)/shard_map/while | solution.py:128
  116.8 102.8 %while.16 = (s32[]{:T(128)}, bf16[3,4,256,128]{2,3,0,1:T(8,128)(2,1)}, bf16[3,4,256,128]{2,3,0,1:T(8,128)(2,1)}, f32[3,12,256,128]{3,1,2,0:T(8,128)}, f32[3,12,2...) while((s32[]{:T(128)}, ...), condition=%wide.region_4.5_spmd, body=%wide.region_0.4_spmd.sunk | while | flops 1345845504 | bytes 72409984 | solution.py:128
  139.7 5.4 %bitcast_dynamic-update-slice_fusion.4 = f32[3,12,256,128]{3,1,2,0:T(8,128)} fusion(f32[3,12,256,128]{3,1,2,0:T(8,128)} %get-tuple-element.231, s32[]{:T(128)S(6)} %copy.106, f32[4,3,256,128]{3,2,1,0:T(8,128)} %fusion.83, s32[4,3]{0,1:T(4,128)S(1)} %copy.96), kind=kOutput, calls=%fused_computation.10.clone.1 | convolution fusion | flops 56623248 | bytes 3670068 | tf_op jit(solution)/shard_map/while/body/eval_jaxpr/anj,ankd->jkd/dot_general | solution.py:94
  174.0 5.4 %bitcast_dynamic-update-slice_fusion.4 = f32[3,12,256,128]{3,1,2,0:T(8,128)} fusion(f32[3,12,256,128]{3,1,2,0:T(8,128)} %get-tuple-element.231, s32[]{:T(128)S(6)} %copy.106, f32[4,3,256,128]{3,2,1,0:T(8,128)} %fusion.83, s32[4,3]{0,1:T(4,128)S(1)} %copy.96), kind=kOutput, calls=%fused_computation.10.clone.1 | convolution fusion | flops 56623248 | bytes 3670068 | tf_op jit(solution)/shard_map/while/body/eval_jaxpr/anj,ankd->jkd/dot_general | solution.py:94
  208.3 5.4 %bitcast_dynamic-update-slice_fusion.4 = f32[3,12,256,128]{3,1,2,0:T(8,128)} fusion(f32[3,12,256,128]{3,1,2,0:T(8,128)} %get-tuple-element.231, s32[]{:T(128)S(6)} %copy.106, f32[4,3,256,128]{3,2,1,0:T(8,128)} %fusion.83, s32[4,3]{0,1:T(4,128)S(1)} %copy.96), kind=kOutput, calls=%fused_computation.10.clone.1 | convolution fusion | flops 56623248 | bytes 3670068 | tf_op jit(solution)/shard_map/while/body/eval_jaxpr/anj,ankd->jkd/dot_general | solution.py:94
  219.6 6.8 %copy.57 = f32[12,256,3,128]{1,0,3,2:T(8,128)} copy(f32[12,256,3,128]{3,0,1,2:T(8,128)} %bitcast.173) | data formatting | bytes 9437184 | tf_op jit(solution)/shard_map/transpose | solution.py:65
  226.3 6.9 %stack_reshape.6 = f32[1,3072,384]{1,2,0:T(8,128)} reshape(f32[12,256,3,128]{1,0,3,2:T(8,128)} %copy.57) | data formatting | bytes 9437184 | tf_op jit(solution)/shard_map/stack;reshape | solution.py:131
  233.2 5.1 %constant_dynamic-update-slice_fusion.3 = f32[2,3072,384]{1,2,0:T(8,128)} fusion(f32[1,3072,384]{1,2,0:T(8,128)} %stack_reshape.6), kind=kLoop, calls=%fused_computation.53 | loop fusion | bytes 9437184
  238.3 6.7 %copy.58 = f32[12,256,3,128]{1,0,3,2:T(8,128)} copy(f32[12,256,3,128]{3,0,1,2:T(8,128)} %bitcast.174) | data formatting | bytes 9437184 | tf_op jit(solution)/shard_map/transpose | solution.py:65
  245.1 6.9 %stack_reshape.7 = f32[1,3072,384]{1,2,0:T(8,128)} reshape(f32[12,256,3,128]{1,0,3,2:T(8,128)} %copy.58) | data formatting | bytes 9437184 | tf_op jit(solution)/shard_map/stack;reshape | solution.py:131
  251.9 5.0 %constant_dynamic-update-slice_fusion.2 = f32[2,3072,384]{1,2,0:T(8,128)} fusion(f32[2,3072,384]{1,2,0:T(8,128)} %constant_dynamic-update-slice_fusion.3, f32[1,3072,384]{1,2,0:T(8,128)} %stack_reshape.7), kind=kLoop, calls=%fused_computation.52 | loop fusion | bytes 9437184 | tf_op jit(solution)/shard_map/stack | solution.py:131
  257.0 4.4 %convert.8 = bf16[2,3072,384]{1,2,0:T(8,128)(2,1)S(1)} convert(f32[2,3072,384]{1,2,0:T(8,128)} %constant_dynamic-update-slice_fusion.2) | non-fusion elementwise | flops 2359296 | bytes 14155776 | tf_op jit(solution)/shard_map/convert.3
  264.1 5.7 %collective-permute-start.5 = (bf16[2,1024,384]{1,2,0:T(8,128)(2,1)S(1)}, bf16[2,1024,384]{1,2,0:T(8,128)(2,1)}, u32[]{:S(2)}, u32[]{:S(2)}) collective-permute-start(bf16[2,1024,384]{1,2,0:T(8,128)(2,1)S(1)} %get-tuple-element.126), channel_id=1, source_target_pairs={{4,0},{8,4},{12,8},{5,1},{9,5},{13,9},{6,2},{10,6},{14,10},{7,3},{... | collective-permute-start | bytes 4718600 | tf_op jit(solution)/shard_map/ppermute | solution.py:53
  273.3 28.5 %collective-permute-done.6 = bf16[2,1024,384]{1,2,0:T(8,128)(2,1)} collective-permute-done((bf16[2,1024,384]{1,2,0:T(8,128)(2,1)}, bf16[2,1024,384]{1,2,0:T(8,128)(2,1)}, u32[]{:S(2)}, u32[]{:S(2)}) %collective-permute-start.6) | collective-permute-done | bytes 1572896 | tf_op jit(solution)/shard_map/ppermute | solution.py:53
  312.8 10.4 %all-to-all-done.5 = bf16[4,256,384]{2,1,0:T(8,128)(2,1)S(1)} async-done(((bf16[4,256,384]{2,1,0:T(8,128)(2,1)}), bf16[4,256,384]{2,1,0:T(8,128)(2,1)S(1)}, u32[]{:S(2)}, u32[]{:S(2)}) %all-to-all-start.5) | async-done | bytes 786464 | tf_op jit(solution)/shard_map/all_to_all | solution.py:140
  329.4 13.2 %collective-permute-done.3 = bf16[1,256,384]{1,2,0:T(8,128)(2,1)} collective-permute-done((bf16[1,256,384]{1,2,0:T(8,128)(2,1)}, bf16[1,256,384]{1,2,0:T(8,128)(2,1)}, u32[]{:S(2)}, u32[]{:S(2)}) %collective-permute-start.3) | collective-permute-done | bytes 196640 | tf_op jit(solution)/shard_map/ppermute | solution.py:28
  (156 shorter events, 154.7 us)
Async XLA Ops:
  0.6 5.9 %copy-start.6 = (bf16[256,1536]{1,0:T(8,128)(2,1)S(1)}, bf16[256,1536]{1,0:T(8,128)(2,1)}, u32[]{:S(2)}) copy-start(bf16[256,1536]{1,0:T(8,128)(2,1)} %param.9) | copy-start | bytes 2359300
  3.0 15.1 %all-to-all-start.2 = ((bf16[256,4,384]{0,2,1:T(8,128)(2,1)}), bf16[256,4,384]{0,2,1:T(8,128)(2,1)S(1)}, u32[]{:S(2)}, u32[]{:S(2)}) async-start(bf16[256,4,384]{0,2,1:T(8,128)(2,1)} %bitcast.33), calls=%async_computation.2 | async-start | bytes 1572864 | tf_op jit(solution)/shard_map/all_to_all | solution.py:106
  18.1 15.1 %all-to-all-start.1 = ((bf16[256,4,384]{0,2,1:T(8,128)(2,1)}), bf16[256,4,384]{0,2,1:T(8,128)(2,1)S(1)}, u32[]{:S(2)}, u32[]{:S(2)}) async-start(bf16[256,4,384]{0,2,1:T(8,128)(2,1)} %bitcast.30), calls=%async_computation.1 | async-start | bytes 1572864 | tf_op jit(solution)/shard_map/all_to_all | solution.py:105
  22.0 17.8 %copy-start.7 = (bf16[256,1536]{1,0:T(8,128)(2,1)S(1)}, bf16[256,1536]{1,0:T(8,128)(2,1)}, u32[]{:S(2)}) copy-start(bf16[256,1536]{1,0:T(8,128)(2,1)} %param.8) | copy-start | bytes 2359300
  33.6 10.8 %copy-start.9 = (s32[16,3]{0,1:T(4,128)S(1)}, s32[16,3]{0,1:T(4,128)}, u32[]{:S(2)}) copy-start(s32[16,3]{0,1:T(4,128)} %param.12) | copy-start | bytes 580
  33.6 10.8 %copy-start.10 = (s32[16,3]{0,1:T(4,128)S(1)}, s32[16,3]{0,1:T(4,128)}, u32[]{:S(2)}) copy-start(s32[16,3]{0,1:T(4,128)} %param.13) | copy-start | bytes 580
  33.6 11.1 %copy-start.8 = (bf16[256,1536]{1,0:T(8,128)(2,1)S(1)}, bf16[256,1536]{1,0:T(8,128)(2,1)}, u32[]{:S(2)}) copy-start(bf16[256,1536]{1,0:T(8,128)(2,1)} %param.11) | copy-start | bytes 2359300
  35.0 36.1 %collective-permute-start.1 = (bf16[2,1024,384]{2,1,0:T(8,128)(2,1)}, bf16[2,1024,384]{2,1,0:T(8,128)(2,1)}, u32[]{:S(2)}, u32[]{:S(2)}) collective-permute-start(bf16[2,1024,384]{2,1,0:T(8,128)(2,1)} %pad_maximum_fusion.1), channel_id=1, source_target_pairs={{4,0},{8,4},{12,8},{5,1},{9,5},{13,9},{6,2},{10,6},{14,10},{7,3},{... | collective-permute-start | bytes 4718600 | tf_op jit(solution)/shard_map/ppermute | solution.py:43
  38.5 37.9 %collective-permute-start = (bf16[2,1024,384]{2,1,0:T(8,128)(2,1)}, bf16[2,1024,384]{2,1,0:T(8,128)(2,1)}, u32[]{:S(2)}, u32[]{:S(2)}) collective-permute-start(bf16[2,1024,384]{2,1,0:T(8,128)(2,1)} %pad_maximum_fusion.1), channel_id=1, source_target_pairs={{0,4},{4,8},{8,12},{1,5},{5,9},{9,13},{2,6},{6,10},{10,14},{3,7},{... | collective-permute-start | bytes 4718600 | tf_op jit(solution)/shard_map/ppermute | solution.py:41
  40.9 40.1 %all-to-all-start = ((bf16[256,4,384]{0,2,1:T(8,128)(2,1)}), bf16[256,4,384]{0,2,1:T(8,128)(2,1)S(1)}, u32[]{:S(2)}, u32[]{:S(2)}) async-start(bf16[256,4,384]{0,2,1:T(8,128)(2,1)} %bitcast.26), calls=%async_computation | async-start | bytes 1572864 | tf_op jit(solution)/shard_map/all_to_all | solution.py:104
  81.0 35.7 %all-to-all-start.3 = ((bf16[256,4,384]{0,2,1:T(8,128)(2,1)}), bf16[256,4,384]{0,2,1:T(8,128)(2,1)}, u32[]{:S(2)}, u32[]{:S(2)}) async-start(bf16[256,4,384]{0,2,1:T(8,128)(2,1)} %bitcast.38), calls=%async_computation.3 | async-start | bytes 1572864 | tf_op jit(solution)/shard_map/all_to_all | solution.py:107
  122.3 2.6 copy-start.2
  147.0 4.1 %copy-start.4 = (bf16[3,4,256,128]{2,3,0,1:T(8,128)(2,1)S(1)}, bf16[3,4,256,128]{2,3,0,1:T(8,128)(2,1)}, u32[]{:S(2)}) copy-start(bf16[3,4,256,128]{2,3,0,1:T(8,128)(2,1)} %copy-done.3) | copy-start | bytes 2359300 | tf_op jit(solution)/shard_map/while
  181.3 4.0 %copy-start.4 = (bf16[3,4,256,128]{2,3,0,1:T(8,128)(2,1)S(1)}, bf16[3,4,256,128]{2,3,0,1:T(8,128)(2,1)}, u32[]{:S(2)}) copy-start(bf16[3,4,256,128]{2,3,0,1:T(8,128)(2,1)} %copy-done.3) | copy-start | bytes 2359300 | tf_op jit(solution)/shard_map/while
  215.5 4.1 %copy-start.4 = (bf16[3,4,256,128]{2,3,0,1:T(8,128)(2,1)S(1)}, bf16[3,4,256,128]{2,3,0,1:T(8,128)(2,1)}, u32[]{:S(2)}) copy-start(bf16[3,4,256,128]{2,3,0,1:T(8,128)(2,1)} %copy-done.3) | copy-start | bytes 2359300 | tf_op jit(solution)/shard_map/while
  262.8 39.0 %collective-permute-start.6 = (bf16[2,1024,384]{1,2,0:T(8,128)(2,1)}, bf16[2,1024,384]{1,2,0:T(8,128)(2,1)}, u32[]{:S(2)}, u32[]{:S(2)}) collective-permute-start(bf16[2,1024,384]{1,2,0:T(8,128)(2,1)} %get-tuple-element.127), channel_id=1, source_target_pairs={{0,4},{4,8},{8,12},{1,5},{5,9},{9,13},{2,6},{6,10},{10,14},{3,7},{... | collective-permute-start | bytes 4718600 | tf_op jit(solution)/shard_map/ppermute | solution.py:53
  264.1 38.5 %collective-permute-start.5 = (bf16[2,1024,384]{1,2,0:T(8,128)(2,1)S(1)}, bf16[2,1024,384]{1,2,0:T(8,128)(2,1)}, u32[]{:S(2)}, u32[]{:S(2)}) collective-permute-start(bf16[2,1024,384]{1,2,0:T(8,128)(2,1)S(1)} %get-tuple-element.126), channel_id=1, source_target_pairs={{4,0},{8,4},{12,8},{5,1},{9,5},{13,9},{6,2},{10,6},{14,10},{7,3},{... | collective-permute-start | bytes 4718600 | tf_op jit(solution)/shard_map/ppermute | solution.py:53
  269.8 37.8 %all-to-all-start.4 = ((bf16[4,256,384]{1,2,0:T(8,128)(2,1)}), bf16[4,256,384]{1,2,0:T(8,128)(2,1)S(1)}, u32[]{:S(2)}, u32[]{:S(2)}) async-start(bf16[4,256,384]{1,2,0:T(8,128)(2,1)} %bitcast.48), calls=%async_computation.4 | async-start | bytes 1572864 | tf_op jit(solution)/shard_map/all_to_all | solution.py:139
  306.3 4.8 %copy-start.5 = (bf16[3,4,256,128]{2,3,0,1:T(8,128)(2,1)S(1)}, bf16[3,4,256,128]{2,3,0,1:T(8,128)(2,1)}, u32[]{:S(2)}) copy-start(bf16[3,4,256,128]{2,3,0,1:T(8,128)(2,1)} %get-tuple-element.64) | copy-start | bytes 2359300
  307.6 15.6 %all-to-all-start.5 = ((bf16[4,256,384]{2,1,0:T(8,128)(2,1)}), bf16[4,256,384]{2,1,0:T(8,128)(2,1)S(1)}, u32[]{:S(2)}, u32[]{:S(2)}) async-start(bf16[4,256,384]{2,1,0:T(8,128)(2,1)} %bitcast.53), calls=%async_computation.5 | async-start | bytes 1572864 | tf_op jit(solution)/shard_map/all_to_all | solution.py:140
  311.2 15.6 %collective-permute-start.2 = (bf16[1,256,384]{1,2,0:T(8,128)(2,1)S(1)}, bf16[1,256,384]{1,2,0:T(8,128)(2,1)S(1)}, u32[]{:S(2)}, u32[]{:S(2)}) collective-permute-start(bf16[1,256,384]{1,2,0:T(8,128)(2,1)S(1)} %constant_dynamic-slice_fusion.2), channel_id=1, source_target_pairs={{0,1},{1,2},{2,3},{3,0},{4,5},{5,6},{6,7},{7,4},{8,9},{9,10},{10,1... | collective-permute-start | bytes 589832 | tf_op jit(solution)/shard_map/ppermute | solution.py:28
  323.2 24.2 %all-to-all-start.6 = ((bf16[4,256,384]{2,1,0:T(8,128)(2,1)}), bf16[4,256,384]{2,1,0:T(8,128)(2,1)S(1)}, u32[]{:S(2)}, u32[]{:S(2)}) async-start(bf16[4,256,384]{2,1,0:T(8,128)(2,1)} %bitcast.56), calls=%async_computation.6 | async-start | bytes 1572864 | tf_op jit(solution)/shard_map/all_to_all | solution.py:143
  327.5 15.1 %collective-permute-start.3 = (bf16[1,256,384]{1,2,0:T(8,128)(2,1)}, bf16[1,256,384]{1,2,0:T(8,128)(2,1)}, u32[]{:S(2)}, u32[]{:S(2)}) collective-permute-start(bf16[1,256,384]{1,2,0:T(8,128)(2,1)} %get-tuple-element.133), channel_id=1, source_target_pairs={{0,2},{1,3},{2,0},{3,1},{4,6},{5,7},{6,4},{7,5},{8,10},{9,11},{10,... | collective-permute-start | bytes 589832 | tf_op jit(solution)/shard_map/ppermute | solution.py:28
  329.4 14.2 %collective-permute-start.4 = (bf16[1,256,384]{1,2,0:T(8,128)(2,1)S(1)}, bf16[1,256,384]{1,2,0:T(8,128)(2,1)S(1)}, u32[]{:S(2)}, u32[]{:S(2)}) collective-permute-start(bf16[1,256,384]{1,2,0:T(8,128)(2,1)S(1)} %get-tuple-element.132), channel_id=1, source_target_pairs={{0,3},{1,0},{2,1},{3,2},{4,7},{5,4},{6,5},{7,6},{8,11},{9,8},{10,9... | collective-permute-start | bytes 589832 | tf_op jit(solution)/shard_map/ppermute | solution.py:28
  (11 other events, 18.3 us)
